TPU v7x, 32 devices: a whole 2x2x4 slice. The times are simulated.
32 devices in a mesh: shard: 16 (over z, x, core), ctx: 2 (over y).
Axes of the slice: x: 2, y: 2, z: 4, core: 2. Of those that a mesh axis runs over, the one named last changes fastest.
Arguments:
- tokens: bfloat16 [8192, 576], P(('shard', 'ctx')), may hold values from -6 to 6
- cotangent: bfloat16 [8192, 576], P(('shard', 'ctx')), may hold values from -6 to 6
- seq_lengths: int32 [16], P('shard'), may hold values from 64 to 512, as said below
- attn_params: float32 [885888], P('shard')
- attn_first: float32 [885888], P('shard'), may hold values from -6 to 6
- attn_second: float32 [885888], P('shard'), may hold values from 1 to 100
- ffn_params: float32 [2654208], P('shard')
- ffn_first: float32 [2654208], P('shard'), may hold values from -6 to 6
- ffn_second: float32 [2654208], P('shard'), may hold values from 1 to 100
Outputs:
- outputs: bfloat16 [8192, 576], P(('shard', 'ctx'))
- grad_tokens: bfloat16 [8192, 576], P(('shard', 'ctx'))
- attn_grad: float32 [885888], P('shard')
- ffn_grad: float32 [2654208], P('shard')
- attn_new: float32 [885888], P('shard')
- attn_first_new: float32 [885888], P('shard')
- attn_second_new: float32 [885888], P('shard')
- ffn_new: float32 [2654208], P('shard')
- ffn_first_new: float32 [2654208], P('shard')
- ffn_second_new: float32 [2654208], P('shard')
Inputs may be any that keep to these rules, and one draw needn't show every extreme that they name: `seq_lengths`: in every draw some sequence fills all 512 slots.
All inputs are finite; a program needn't handle non-finite values.
Results may differ from a plain program's by a relative error of at most 0.01.
The roundings to bfloat16 on the way count: a program that leaves them out, or rounds other values in their place, can miss the bound.
Values may be sent and summed in bfloat16 or wider, within the bound.
A program may use at most 128 MiB of HBM per device.

v0:
```python
import math
import jax
import jax.numpy as jnp
from jax import lax
from jax.sharding import PartitionSpec as P

MODEL_WIDTH = 576
QUERY_HEADS = 9
KEY_VALUE_HEADS = 3
HEAD_SIZE = 64
FF = 1536
ADAM_STEP = 3
rms_eps = 1e-05
rope_base = 100000.0
beta_one = 0.9
beta_two = 0.95
learn_rate = 0.02
decay_rate = 0.1
adam_eps = 1e-08
masked_score = -1e30


def split_flattened(flattened, shapes):
    pieces = []
    offset = 0
    for shape in shapes:
        width = 1
        for extent in shape:
            width = width * extent
        pieces.append(flattened[offset : offset + width].reshape(shape))
        offset = offset + width
    return pieces


def split_attention(flattened):
    return split_flattened(
        flattened,
        (
            (MODEL_WIDTH, QUERY_HEADS * HEAD_SIZE),
            (MODEL_WIDTH, KEY_VALUE_HEADS * HEAD_SIZE),
            (MODEL_WIDTH, KEY_VALUE_HEADS * HEAD_SIZE),
            (QUERY_HEADS * HEAD_SIZE, MODEL_WIDTH),
            (MODEL_WIDTH,),
            (MODEL_WIDTH,),
        ),
    )


def split_feedforward(flattened):
    return split_flattened(flattened, ((MODEL_WIDTH, FF), (MODEL_WIDTH, FF), (FF, MODEL_WIDTH)))


def rope_tables(positions):
    index = jnp.arange(HEAD_SIZE // 2).astype(jnp.float32)
    inverse = jnp.exp(index * (-2.0 * math.log(rope_base) / HEAD_SIZE))
    angles = positions.astype(jnp.float32)[:, None] * inverse[None, :]
    angles = jnp.concatenate([angles, angles], axis=1)
    return (jnp.cos(angles), jnp.sin(angles))


def apply_rotation(values, cosine_table, sine_table):
    half = values.shape[-1] // 2
    turned = jnp.concatenate([-values[..., half:], values[..., :half]], axis=-1)
    return values * cosine_table[:, None, :] + turned * sine_table[:, None, :]


def reverse_rotation(grads, cosine_table, sine_table):
    half = grads.shape[-1] // 2
    weighted = grads * sine_table[:, None, :]
    turned = jnp.concatenate([weighted[..., half:], -weighted[..., :half]], axis=-1)
    return grads * cosine_table[:, None, :] + turned


def norm_rows(values, gain):
    mean_sq = jnp.mean(values * values, axis=-1, keepdims=True)
    inverse = lax.rsqrt(mean_sq + rms_eps)
    scaled = values * inverse
    return (scaled, inverse, (scaled * gain).astype(jnp.bfloat16))


def norm_back(grad_normed, scaled, inverse, gain):
    grad_scaled = grad_normed * gain
    grad_gain = jnp.sum(grad_normed * scaled, axis=0)
    inner = jnp.mean(grad_scaled * scaled, axis=-1, keepdims=True)
    return (inverse * (grad_scaled - scaled * inner), grad_gain)


def attend(query_rows, keys, values, mask):
    row_entries = query_rows.shape[0]
    scale = 1.0 / math.sqrt(HEAD_SIZE)
    grouped_heads = query_rows.reshape(
        row_entries, KEY_VALUE_HEADS, QUERY_HEADS // KEY_VALUE_HEADS, HEAD_SIZE
    )
    scores = (
        jnp.einsum("tkgd,skd->kgts", grouped_heads, keys, preferred_element_type=jnp.float32)
        * scale
    )
    scores = jnp.where(mask[None, None], scores, masked_score)
    top = jnp.max(scores, axis=-1, keepdims=True)
    total = jnp.sum(jnp.exp(scores - top), axis=-1, keepdims=True)
    log_total = top + jnp.log(total)
    probs = jnp.exp(scores - log_total).astype(jnp.bfloat16)
    mixture = jnp.einsum("kgts,skd->tkgd", probs, values, preferred_element_type=jnp.float32)
    return (mixture.reshape(row_entries, QUERY_HEADS * HEAD_SIZE).astype(jnp.bfloat16), log_total)


def attend_back(query_rows, keys, values, mask, log_total, mixture, mixture_gradient):
    row_entries = query_rows.shape[0]
    head_group = QUERY_HEADS // KEY_VALUE_HEADS
    scale = 1.0 / math.sqrt(HEAD_SIZE)
    grouped_queries = query_rows.reshape(
        row_entries, KEY_VALUE_HEADS, head_group, HEAD_SIZE
    ).transpose(1, 0, 2, 3)
    gradient_groups = mixture_gradient.reshape(
        row_entries, KEY_VALUE_HEADS, head_group, HEAD_SIZE
    ).transpose(1, 0, 2, 3)
    mixture_groups = mixture.reshape(row_entries, KEY_VALUE_HEADS, head_group, HEAD_SIZE).transpose(
        1, 0, 2, 3
    )
    key_groups = keys.transpose(1, 0, 2)
    value_groups = values.transpose(1, 0, 2)

    def one_group(item):
        query_one, key_one, value_one, total_one, mixed_one, grad_one = item
        scores = (
            jnp.einsum("tgd,sd->gts", query_one, key_one, preferred_element_type=jnp.float32)
            * scale
        )
        scores = jnp.where(mask[None], scores, masked_score)
        probs = jnp.exp(scores - total_one)
        delta = jnp.einsum("tgd,tgd->gt", grad_one, mixed_one, preferred_element_type=jnp.float32)
        grad_probs = jnp.einsum(
            "tgd,sd->gts", grad_one, value_one, preferred_element_type=jnp.float32
        )
        grad_scores = (probs * (grad_probs - delta[..., None]) * scale).astype(jnp.bfloat16)
        grad_query = jnp.einsum(
            "gts,sd->tgd", grad_scores, key_one, preferred_element_type=jnp.float32
        )
        key_gradient = jnp.einsum(
            "gts,tgd->sd", grad_scores, query_one, preferred_element_type=jnp.float32
        )
        value_gradient = jnp.einsum(
            "gts,tgd->sd", probs.astype(jnp.bfloat16), grad_one, preferred_element_type=jnp.float32
        )
        return (grad_query, key_gradient, value_gradient)

    grad_query, key_gradient, value_gradient = lax.map(
        one_group,
        (grouped_queries, key_groups, value_groups, log_total, mixture_groups, gradient_groups),
    )
    grad_query = grad_query.transpose(1, 0, 2, 3).reshape(row_entries, QUERY_HEADS, HEAD_SIZE)
    return (grad_query, key_gradient.transpose(1, 0, 2), value_gradient.transpose(1, 0, 2))


def adam_update(params, first, second, grads):
    first_new = beta_one * first + (1.0 - beta_one) * grads
    second_new = beta_two * second + (1.0 - beta_two) * grads * grads
    corr_one = 1.0 - beta_one**ADAM_STEP
    corr_two = 1.0 - beta_two**ADAM_STEP
    moved = first_new / corr_one / (jnp.sqrt(second_new / corr_two) + adam_eps)
    return (params - learn_rate * (moved + decay_rate * params), first_new, second_new)


def owner_layout(term, owners, pair):
    columns = term.shape[0] // owners
    padded_columns = columns + -columns % pair
    table = term.reshape(owners, columns)
    return (jnp.pad(table, ((0, 0), (0, padded_columns - columns))).reshape(-1), columns)


def body(
    tokens,
    cotangent,
    seq_lengths,
    attn_params,
    attn_first,
    attn_second,
    ffn_params,
    ffn_first,
    ffn_second,
):
    row_entries = tokens.shape[0]
    ctx_count = lax.axis_size("ctx")
    ctx_index = lax.axis_index("ctx")
    owners = lax.axis_size("shard")
    slot_entries = row_entries * ctx_count
    length = seq_lengths[0]
    low_params = (attn_params.astype(jnp.bfloat16), ffn_params.astype(jnp.bfloat16))
    attn_whole, ffn_whole = (
        lax.all_gather(low_params[0], "shard", axis=0, tiled=True),
        lax.all_gather(low_params[1], "shard", axis=0, tiled=True),
    )
    w_query, key_matrix, value_matrix, w_out, gain_one, gain_two = split_attention(attn_whole)
    w_gate, w_up, w_down = split_feedforward(ffn_whole)
    gain_one = gain_one.astype(jnp.float32)
    gain_two = gain_two.astype(jnp.float32)
    positions = ctx_index * row_entries + jnp.arange(row_entries)
    key_positions = jnp.arange(slot_entries)
    valid = (positions < length).astype(jnp.float32)[:, None]
    has_rows = ctx_index * row_entries < length
    mask = (key_positions[None, :] <= positions[:, None]) & (key_positions[None, :] < length)
    inputs = tokens.astype(jnp.float32)
    scaled_one, inv_one, first_normed = norm_rows(inputs, gain_one)
    query_raw = jnp.dot(first_normed, w_query, preferred_element_type=jnp.float32).reshape(
        row_entries, QUERY_HEADS, HEAD_SIZE
    )
    unrotated_key = jnp.dot(first_normed, key_matrix, preferred_element_type=jnp.float32).reshape(
        row_entries, KEY_VALUE_HEADS, HEAD_SIZE
    )
    value_reduced = jnp.dot(first_normed, value_matrix, preferred_element_type=jnp.float32).astype(
        jnp.bfloat16
    )
    cosine_table, sine_table = rope_tables(positions)
    query_low = apply_rotation(query_raw, cosine_table, sine_table).astype(jnp.bfloat16)
    key_reduced = (
        apply_rotation(unrotated_key, cosine_table, sine_table)
        .astype(jnp.bfloat16)
        .reshape(row_entries, KEY_VALUE_HEADS * HEAD_SIZE)
    )
    full_keys, full_values = (
        lax.all_gather(key_reduced, "ctx", axis=0, tiled=True),
        lax.all_gather(value_reduced, "ctx", axis=0, tiled=True),
    )
    full_keys = full_keys.reshape(slot_entries, KEY_VALUE_HEADS, HEAD_SIZE)
    full_values = full_values.reshape(slot_entries, KEY_VALUE_HEADS, HEAD_SIZE)
    mixture, log_total = lax.cond(
        has_rows,
        lambda: attend(query_low, full_keys, full_values, mask),
        lambda: (
            jnp.zeros((row_entries, QUERY_HEADS * HEAD_SIZE), jnp.bfloat16),
            jnp.zeros(
                (KEY_VALUE_HEADS, QUERY_HEADS // KEY_VALUE_HEADS, row_entries, 1), jnp.float32
            ),
        ),
    )
    hidden = inputs + jnp.dot(mixture, w_out, preferred_element_type=jnp.float32)
    scaled_two, inv_two, normed_two = norm_rows(hidden, gain_two)
    gate = jnp.dot(normed_two, w_gate, preferred_element_type=jnp.float32)
    upward = jnp.dot(normed_two, w_up, preferred_element_type=jnp.float32)
    sigma = jax.nn.sigmoid(gate)
    activ = (gate * sigma * upward).astype(jnp.bfloat16)
    result = hidden + jnp.dot(activ, w_down, preferred_element_type=jnp.float32)
    outputs = (valid * result).astype(jnp.bfloat16)
    grad_result = valid * cotangent.astype(jnp.float32)
    grad_low = grad_result.astype(jnp.bfloat16)
    grad_w_down = jnp.dot(activ.T, grad_low, preferred_element_type=jnp.float32)
    grad_activ = jnp.dot(grad_low, w_down.T, preferred_element_type=jnp.float32)
    grad_gate = (grad_activ * upward * sigma * (1.0 + gate * (1.0 - sigma))).astype(jnp.bfloat16)
    grad_upward = (grad_activ * gate * sigma).astype(jnp.bfloat16)
    grad_w_gate = jnp.dot(normed_two.T, grad_gate, preferred_element_type=jnp.float32)
    grad_w_up = jnp.dot(normed_two.T, grad_upward, preferred_element_type=jnp.float32)
    ffn_term = jnp.concatenate(
        [grad_w_gate.reshape(-1), grad_w_up.reshape(-1), grad_w_down.reshape(-1)]
    )
    ffn_padded, ffn_columns = owner_layout(ffn_term, owners, ctx_count)
    grad_normed_two = jnp.dot(grad_gate, w_gate.T, preferred_element_type=jnp.float32) + jnp.dot(
        grad_upward, w_up.T, preferred_element_type=jnp.float32
    )
    grad_hidden_part, grad_gain_two = norm_back(grad_normed_two, scaled_two, inv_two, gain_two)
    grad_hidden = grad_result + grad_hidden_part
    grad_hidden_low = grad_hidden.astype(jnp.bfloat16)
    grad_w_out = jnp.dot(mixture.T, grad_hidden_low, preferred_element_type=jnp.float32)
    mixture_gradient = jnp.dot(grad_hidden_low, w_out.T, preferred_element_type=jnp.float32).astype(
        jnp.bfloat16
    )
    grad_query, full_key_gradient, full_value_gradient = lax.cond(
        has_rows,
        lambda: attend_back(
            query_low, full_keys, full_values, mask, log_total, mixture, mixture_gradient
        ),
        lambda: (
            jnp.zeros((row_entries, QUERY_HEADS, HEAD_SIZE), jnp.float32),
            jnp.zeros((slot_entries, KEY_VALUE_HEADS, HEAD_SIZE), jnp.float32),
            jnp.zeros((slot_entries, KEY_VALUE_HEADS, HEAD_SIZE), jnp.float32),
        ),
    )
    key_gradient, value_gradient = (
        lax.psum_scatter(
            full_key_gradient.reshape(slot_entries, KEY_VALUE_HEADS * HEAD_SIZE),
            "ctx",
            scatter_dimension=0,
            tiled=True,
        ),
        lax.psum_scatter(
            full_value_gradient.reshape(slot_entries, KEY_VALUE_HEADS * HEAD_SIZE),
            "ctx",
            scatter_dimension=0,
            tiled=True,
        ),
    )
    grad_query_raw = (
        reverse_rotation(grad_query, cosine_table, sine_table)
        .astype(jnp.bfloat16)
        .reshape(row_entries, QUERY_HEADS * HEAD_SIZE)
    )
    unrotated_key_gradient = (
        reverse_rotation(
            key_gradient.reshape(row_entries, KEY_VALUE_HEADS, HEAD_SIZE), cosine_table, sine_table
        )
        .astype(jnp.bfloat16)
        .reshape(row_entries, KEY_VALUE_HEADS * HEAD_SIZE)
    )
    plain_value_gradient = value_gradient.astype(jnp.bfloat16)
    grad_w_query = jnp.dot(first_normed.T, grad_query_raw, preferred_element_type=jnp.float32)
    grad_w_key = jnp.dot(first_normed.T, unrotated_key_gradient, preferred_element_type=jnp.float32)
    grad_w_value = jnp.dot(first_normed.T, plain_value_gradient, preferred_element_type=jnp.float32)
    grad_normed_one = jnp.dot(grad_query_raw, w_query.T, preferred_element_type=jnp.float32)
    grad_normed_one = grad_normed_one + jnp.dot(
        unrotated_key_gradient, key_matrix.T, preferred_element_type=jnp.float32
    )
    grad_normed_one = grad_normed_one + jnp.dot(
        plain_value_gradient, value_matrix.T, preferred_element_type=jnp.float32
    )
    grad_input_part, grad_gain_one = norm_back(grad_normed_one, scaled_one, inv_one, gain_one)
    grad_tokens = (grad_hidden + grad_input_part).astype(jnp.bfloat16)
    attn_term = jnp.concatenate(
        [
            grad_w_query.reshape(-1),
            grad_w_key.reshape(-1),
            grad_w_value.reshape(-1),
            grad_w_out.reshape(-1),
            grad_gain_one,
            grad_gain_two,
        ]
    )
    attn_padded, attn_columns = owner_layout(attn_term, owners, ctx_count)
    attn_half, ffn_half = (
        lax.psum_scatter(attn_padded, ("shard", "ctx"), scatter_dimension=0, tiled=True),
        lax.psum_scatter(ffn_padded, ("shard", "ctx"), scatter_dimension=0, tiled=True),
    )
    attn_joined, ffn_joined = (
        lax.all_gather(attn_half, "ctx", axis=0, tiled=True),
        lax.all_gather(ffn_half, "ctx", axis=0, tiled=True),
    )
    attn_grad = attn_joined[:attn_columns]
    attn_new, attn_first_new, attn_second_new = adam_update(
        attn_params, attn_first, attn_second, attn_grad
    )
    ffn_new, ffn_first_new, ffn_second_new = adam_update(
        ffn_params, ffn_first, ffn_second, ffn_joined
    )
    return (
        outputs,
        grad_tokens,
        attn_grad,
        ffn_joined,
        attn_new,
        attn_first_new,
        attn_second_new,
        ffn_new,
        ffn_first_new,
        ffn_second_new,
    )


def solution(mesh):
    return jax.shard_map(
        body,
        mesh=mesh,
        in_specs=(
            P(("shard", "ctx"), None),
            P(("shard", "ctx"), None),
            P("shard"),
            P("shard"),
            P("shard"),
            P("shard"),
            P("shard"),
            P("shard"),
            P("shard"),
        ),
        out_specs=(
            P(("shard", "ctx"), None),
            P(("shard", "ctx"), None),
            P("shard"),
            P("shard"),
            P("shard"),
            P("shard"),
            P("shard"),
            P("shard"),
            P("shard"),
            P("shard"),
        ),
        check_vma=False,
    )
```

profile of v0, /device:TPU:0, one launch (start us, length us, event | category | flops | bytes accessed | tf_op | source)
XLA Modules:
  0.0 597.9 jit_solution(964759938562371816)
XLA Ops:
  16.1 95.9 %all-reduce.9.cloned.1.call-done = bf16[885888]{0:T(1024)(128)(2,1)} async-done(((bf16[885888]{0:T(1024)(128)(2,1)}), bf16[885888]{0:T(1024)(128)(2,1)}) %all-reduce.9.cloned.1.call-update) | async-done | bytes 1771792
  112.0 1.4 fusion.89
  119.5 5.3 all_gather.19
  125.2 5.3 all_gather.20
  131.9 4.6 conditional.2
  134.5 2.0 fusion.3
  137.3 33.6 %all-gather.2.cloned.1.call-done = bf16[2654208]{0:T(1024)(128)(2,1)} async-done(((bf16[165888]{0:T(1024)(128)(2,1)}), bf16[2654208]{0:T(1024)(128)(2,1)}) %all-gather.2.cloned.1.call-update) | async-done | bytes 5308432 | tf_op jit(solution)/shard_map/all_gather | solution.py:191
  170.9 4.7 fusion.88
  175.6 3.0 slice.124
  178.6 3.6 slice.126
  182.1 3.4 fusion.93
  185.6 2.0 fusion.94
  187.5 4.3 slice.128
  191.9 4.8 multiply_convert_fusion
  200.2 1.6 fusion.69
  201.8 27.9 %conditional.3 = (f32[256,9,64]{0,2,1:T(8,128)}, f32[512,3,64]{0,2,1:T(8,128)}, f32[512,3,64]{0,2,1:T(8,128)}) conditional(s32[]{:T(128)} %convert_element_type.112, () %tuple.30, (bf16[256,9,64]{0,2,1:T(8,128)(2,1)S(1)}, bf16[512,3,64]{0,2,1:T(8,128)(2,1)}, bf16[512,3,64]{0,2,1:T(8,128)(2,1)}, bf16[256,576]{0,1:T(8,128)(2,1)S(1)}, ...), branch_computations={%region_7.8_spmd, %region_8.0_spmd} | conditional | flops 254999808 | bytes 16739761 | solution.py:266
  201.8 27.9 %while.13 = (s32[]{:T(128)}, f32[3,256,3,64]{1,3,2,0:T(8,128)}, f32[3,512,64]{1,2,0:T(8,128)}, f32[3,512,64]{1,2,0:T(8,128)}, bf16[3,512,64]{1,2,0:T(8,128)(2,1)...) while((s32[]{:T(128)}, f32[3,256,3,64]{1,3,2,0:T(8,128)}, ...), condition=%wide.region_10.10_spmd, body=%wide.region_9.9_spmd.sunk | while | flops 254999808 | bytes 16739633 | solution.py:147
  202.5 1.5 fusion.157
  205.8 1.4 fusion.158
  207.2 1.8 fusion.159
  211.8 1.5 fusion.157
  215.1 1.4 fusion.158
  216.5 1.8 fusion.159
  221.1 1.5 fusion.157
  224.4 1.4 fusion.158
  225.8 1.8 fusion.159
  231.2 2.7 fusion.61
  236.2 1.7 reshape.293
  238.0 1.9 reshape.296
  239.9 5.4 reshape.299
  245.3 2.4 fusion.97
  247.6 4.6 reshape.298
  252.3 2.4 fusion.96
  254.7 4.6 reshape.297
  259.3 11.2 %pad_maximum_fusion = f32[2654208]{0:T(1024)} fusion(f32[884736]{0:T(1024)} %reshape.299, f32[884736]{0:T(1024)} %reshape.298, f32[884736]{0:T(1024)} %reshape.297), kind=kLoop, calls=%fused_computation.50 | loop fusion | flops 5308416 | bytes 21233664 | tf_op jit(solution)/shard_map/concatenate | solution.py:252
  274.4 2.1 reshape.294
  278.9 2.0 fusion.74
  280.9 2.3 reshape.295
  283.2 2.9 fusion.50
  286.1 25.4 %concatenate.37 = f32[885888]{0:T(1024)} concatenate(f32[331776]{0:T(1024)S(1)} %copy-done.16, f32[110592]{0:T(1024)} %reshape.294, f32[110592]{0:T(1024)} %reshape.295, f32[331776]{0:T(1024)S(1)} %reshape.296, f32[576]{0:T(1024)S(1)} %get-tuple-element.157, f32[576]{0:T(1024)S(1)} %copy-done.48), dimensions={0} | concatenate | bytes 7087104 | tf_op jit(solution)/shard_map/concatenate | solution.py:316
  313.4 2.8 fusion.38
  317.2 242.8 %all-reduce.13.cloned.1.call-done = (f32[885888]{0:T(1024)}, f32[2654208]{0:T(1024)}) async-done(((f32[885888]{0:T(1024)}, f32[2654208]{0:T(1024)}), (f32[885888]{0:T(1024)}, f32[2654208]{0:T(1024)})) %all-reduce.13.cloned.1.call-update) | async-done | bytes 14160400
  560.1 1.4 dynamic-slice_dynamic-update-slice_fusion
  563.3 12.8 %all_gather.23 = f32[165888]{0:T(1024)S(1)} all-gather(f32[82944]{0:T(1024)S(1)} %dynamic-slice.3), channel_id=1, replica_groups=mesh['shard'=16,'ctx'=2] {'ctx'}, dimensions={0}, use_global_device_ids=true | all-gather | bytes 995328 | tf_op jit(solution)/shard_map/all_gather | solution.py:333
  576.1 1.6 multiply_subtract_fusion
  577.7 8.9 %all-reduce.11.cloned.1.call-done = f32[55368]{0:T(1024)} async-done(((f32[55368]{0:T(1024)}), f32[55368]{0:T(1024)}) %all-reduce.11.cloned.1.call-update) | async-done | bytes 221488
  586.6 1.9 multiply_subtract_fusion.1
  588.5 1.6 copy.105
  (234 shorter events, 50.2 us)
Async XLA Ops:
  7.2 104.9 %all-reduce.9.cloned.1.call-start = ((), (), s32[]{:S(2)}) async-start(), calls=%async_computation.5 | async-start | bytes 3547136
  10.1 2.7 copy-start.26
  10.2 4.1 copy-start
  12.7 158.1 %all-gather.2.cloned.1.call-start = ((), (), s32[]{:S(2)}) async-start(), calls=%async_computation.2 | async-start | bytes 5640192 | tf_op jit(solution)/shard_map/all_gather | solution.py:191
  13.6 257.0 %reduce-scatter.3.cloned.1.call-start = ((), (), s32[]{:S(2)}) async-start(), calls=%async_computation.3 | async-start | bytes 589824 | tf_op jit(solution)/shard_map/reduce_scatter | solution.py:278
  14.7 116.4 %copy-start.32 = (f32[256,64]{0,1:T(8,128)}, f32[256,64]{0,1:T(8,128)S(1)}, u32[]{:S(2)}) copy-start(f32[256,64]{0,1:T(8,128)S(1)} %get-tuple-element.211) | copy-start | bytes 196612
  14.7 116.4 %copy-start.34 = (f32[256,64]{0,1:T(8,128)}, f32[256,64]{0,1:T(8,128)S(1)}, u32[]{:S(2)}) copy-start(f32[256,64]{0,1:T(8,128)S(1)} %get-tuple-element.212) | copy-start | bytes 196612
  114.0 2.7 copy-start.12
  115.7 3.8 copy-start.28
  116.7 8.1 %copy-start.38 = (bf16[576,192]{1,0:T(8,128)(2,1)}, bf16[576,192]{1,0:T(8,128)(2,1)S(1)}, u32[]{:S(2)}) copy-start(bf16[576,192]{1,0:T(8,128)(2,1)S(1)} %reshape.286) | copy-start | bytes 663556
  117.3 19.3 %copy-start.10 = (bf16[576,576]{1,0:T(8,128)(2,1)}, bf16[576,576]{1,0:T(8,128)(2,1)S(1)}, u32[]{:S(2)}) copy-start(bf16[576,576]{1,0:T(8,128)(2,1)S(1)} %reshape.288) | copy-start | bytes 1990660
  124.8 7.1 %copy-start.30 = (bf16[512,192]{0,1:T(8,128)(2,1)}, bf16[512,192]{0,1:T(8,128)(2,1)S(1)}, u32[]{:S(2)}) copy-start(bf16[512,192]{0,1:T(8,128)(2,1)S(1)} %all_gather.19) | copy-start | bytes 589828
  137.2 48.3 %copy-start.7 = (bf16[256,576]{0,1:T(8,128)(2,1)}, bf16[256,576]{0,1:T(8,128)(2,1)S(1)}, u32[]{:S(2)}) copy-start(bf16[256,576]{0,1:T(8,128)(2,1)S(1)} %multiply_convert_fusion.3) | copy-start | bytes 884740
  187.5 4.3 copy-start.39
  191.9 4.8 copy-start.1
  201.8 2.5 copy-start.17
  205.8 3.2 copy-start.18
  205.8 4.3 copy-start.3
  207.2 3.9 copy-start.15
  211.1 2.5 copy-start.17
  215.1 3.2 copy-start.18
  215.1 4.3 copy-start.3
  216.5 3.9 copy-start.15
  224.4 3.2 copy-start.18
  224.4 4.3 copy-start.3
  225.8 3.9 copy-start.15
  229.7 49.2 %reduce-scatter.5.cloned.1.call-start = ((), (), s32[]{:S(2)}) async-start(), calls=%async_computation.4 | async-start | bytes 589824 | tf_op jit(solution)/shard_map/reduce_scatter | solution.py:284
  231.2 2.7 copy-start.33
  239.9 5.4 copy-start.8
  239.9 5.4 copy-start.20
  247.6 4.7 copy-start.22
  259.3 11.3 %copy-start.35 = (f32[256,64]{0,1:T(8,128)S(1)}, f32[256,64]{0,1:T(8,128)}, u32[]{:S(2)}) copy-start(f32[256,64]{0,1:T(8,128)} %copy-done.34) | copy-start | bytes 196612
  259.3 300.8 %all-reduce.13.cloned.1.call-start = ((), (), s32[]{:S(2)}) async-start(), calls=%async_computation.7 | async-start | bytes 28327936
  271.5 5.0 copy-start.29
  271.6 6.1 %copy-start.13 = (bf16[576,576]{1,0:T(8,128)(2,1)S(1)}, bf16[576,576]{1,0:T(8,128)(2,1)}, u32[]{:S(2)}) copy-start(bf16[576,576]{1,0:T(8,128)(2,1)} %copy-done.12) | copy-start | bytes 1990660
  271.6 6.1 %copy-start.25 = (bf16[256,9,64]{0,2,1:T(8,128)(2,1)S(1)}, bf16[256,9,64]{0,2,1:T(8,128)(2,1)}, u32[]{:S(2)}) copy-start(bf16[256,9,64]{0,2,1:T(8,128)(2,1)} %copy-done.24) | copy-start | bytes 884740
  280.9 5.2 copy-start.16
  280.9 5.2 copy-start.48
  311.5 275.1 %all-reduce.11.cloned.1.call-start = ((), (), s32[]{:S(2)}) async-start(), calls=%async_computation.6 | async-start | bytes 450560
  313.4 2.9 copy-start.52
  313.4 2.9 copy-start.5
  313.4 2.9 copy-start.31
  316.3 259.8 %copy-start.27 = (f32[165888]{0:T(1024)S(1)}, f32[165888]{0:T(1024)}, u32[]{:S(2)}) copy-start(f32[165888]{0:T(1024)} %param.21) | copy-start | bytes 1990660
  316.3 259.8 %copy-start.44 = (f32[165888]{0:T(1024)S(1)}, f32[165888]{0:T(1024)}, u32[]{:S(2)}) copy-start(f32[165888]{0:T(1024)} %param.22) | copy-start | bytes 1990660
  316.3 259.7 %copy-start.45 = (f32[165888]{0:T(1024)S(1)}, f32[165888]{0:T(1024)}, u32[]{:S(2)}) copy-start(f32[165888]{0:T(1024)} %param.23) | copy-start | bytes 1990660
  576.1 10.6 %copy-start.41 = (f32[55368]{0:T(1024)S(1)}, f32[55368]{0:T(1024)}, u32[]{:S(2)}) copy-start(f32[55368]{0:T(1024)} %param.18) | copy-start | bytes 664420
  576.1 10.6 %copy-start.46 = (f32[55368]{0:T(1024)S(1)}, f32[55368]{0:T(1024)}, u32[]{:S(2)}) copy-start(f32[55368]{0:T(1024)} %param.19) | copy-start | bytes 664420
  576.1 10.6 %copy-start.47 = (f32[55368]{0:T(1024)S(1)}, f32[55368]{0:T(1024)}, u32[]{:S(2)}) copy-start(f32[55368]{0:T(1024)} %param.20) | copy-start | bytes 664420
  (24 other events, 38.9 us)
Sparse Core Ops, SparseCore 0:
  12.9 99.1 all-reduce.8
  114.8 56.0 all-gather.1
  229.8 11.7 reduce-scatter.2
  259.4 11.7 reduce-scatter.4
  311.7 248.3 all-reduce.12
  562.8 23.7 all-reduce.10
where the time goes:
time: 600 us; the launch traced here: 598 us
  waiting for transfers between devices  381 us (64%)
  local copies, waits for them, and re-layouts  88.9 us (15%)
  matrix products  58.9 us (10%)
  other arithmetic  27.6 us (5%)
  blocking collectives  23.4 us (4%)
  between operations  16.8 us (3%)
    unnamed x9, waiting for transfers between devices  348 us
    all_gather x1, waiting for transfers between devices, body(): lax.all_gather(low_params[1], 'shard', axis=0, tiled=True)  33.6 us
    concatenate x1, local copies, waits for them, and re-layouts, body(): jnp.concatenate([grad_w_query.reshape(-1), grad_w_key.reshape(-1), grad_w...  25.4 us
    slice x6, local copies, waits for them, and re-layouts, split_flattened(): pieces.append(flattened[offset:offset + width].reshape(shape))  18 us
    unnamed x105, local copies, waits for them, and re-layouts  13.8 us
    all_gather x1, blocking collectives, body(): lax.all_gather(ffn_half, 'ctx', axis=0, tiled=True)  12.8 us
  transfers between devices with their start and end apart: 6, of which 4 were waited for; matrix products, arithmetic and copies ran while one was open for 12% of the time, Pallas kernels for 0%

commit v1 on v0

--- a/solution.py
+++ b/solution.py
@@ -18,6 +18,28 @@
 decay_rate = 0.1
 adam_eps = 1e-08
 masked_score = -1e30
+
+
+def in_order(tiles, dim):
+    lengths = list(tiles.shape[1:])
+    lengths[dim] *= tiles.shape[0]
+    return jnp.moveaxis(tiles, 0, dim).reshape(lengths)
+
+
+def collect(x, axis, dim):
+    size = lax.axis_size(axis)
+    pairs = [(i, (i + 1) % size) for i in range(size)]
+    back = [(b, a) for a, b in pairs]
+    lower, upper = ([], [])
+    for step in range(size - 1):
+        if step % 2 == 0:
+            lower.append(lax.ppermute(lower[-1] if lower else x, axis, pairs))
+        else:
+            upper.append(lax.ppermute(upper[-1] if upper else x, axis, back))
+    tiles = jnp.stack([*lower[::-1], x, *upper])
+    shift = lax.axis_index(axis) - len(lower)
+    tiles = tiles[(jnp.arange(size) - shift) % size]
+    return in_order(tiles, dim)
 
 
 def split_flattened(flattened, shapes):
@@ -188,7 +210,7 @@
     low_params = (attn_params.astype(jnp.bfloat16), ffn_params.astype(jnp.bfloat16))
     attn_whole, ffn_whole = (
         lax.all_gather(low_params[0], "shard", axis=0, tiled=True),
-        lax.all_gather(low_params[1], "shard", axis=0, tiled=True),
+        collect(low_params[1], "shard", 0),
     )
     w_query, key_matrix, value_matrix, w_out, gain_one, gain_two = split_attention(attn_whole)
     w_gate, w_up, w_down = split_feedforward(ffn_whole)

time: 600 us -> 689 us (1.15); the launches traced: 598 us -> 675 us
  local copies, waits for them, and re-layouts: 88.9 us -> 171 us
  waiting for transfers between devices: 381 us -> 345 us
  starting transfers between devices: 0.47 us -> 30.6 us
    another operation x0 -> x17, local copies, waits for them, and re-layouts: none -> 56.1 us  [collect(): tiles = jnp.stack([*lower[::-1], x, *upper])]
    all_gather x1 -> x0, waiting for transfers between devices: 33.6 us -> none  [body(): lax.all_gather(low_params[1], 'shard', axis=0, tiled=True)]
    ppermute x0 -> x15, starting transfers between devices: none -> 30.4 us  [the longest x7 29.3 us: collect(): upper.append(lax.ppermute(upper[-1] if upper else x, axis, back))]
    unnamed x9 -> x8, waiting for transfers between devices: 348 us -> 329 us
    gather x0 -> x3, local copies, waits for them, and re-layouts: none -> 16.7 us  [collect(): tiles = tiles[(jnp.arange(size) - shift) % size]]
    ppermute x0 -> x15, waiting for transfers between devices: none -> 16.6 us  [the longest x8 14.6 us: collect(): lower.append(lax.ppermute(lower[-1] if lower else x, axis, pairs))]
    slice x6 -> x4, local copies, waits for them, and re-layouts: 18 us -> 24.7 us  [split_flattened(): pieces.append(flattened[offset:offset + width].reshape(shape))]
  transfers between devices with their start and end apart: 6 -> 20, of which waited for: 4 -> 9; matrix products, arithmetic and copies ran while one was open for 12% -> 15% of each run, Pallas kernels for 0% -> 0%
where the time goes in v1:
time: 689 us; the launch traced here: 675 us
  waiting for transfers between devices  345 us (50%)
  local copies, waits for them, and re-layouts  171 us (25%)
  matrix products  56.2 us (8%)
  other arithmetic  30.7 us (4%)
  starting transfers between devices  30.6 us (4%)
  blocking collectives  24.7 us (4%)
  between operations  16.7 us (2%)
    unnamed x8, waiting for transfers between devices  329 us
    another operation x17, local copies, waits for them, and re-layouts, collect(): tiles = jnp.stack([*lower[::-1], x, *upper])  56.1 us
    ppermute x7, starting transfers between devices, collect(): upper.append(lax.ppermute(upper[-1] if upper else x, axis, back))  29.3 us
    concatenate x1, local copies, waits for them, and re-layouts, body(): jnp.concatenate([grad_w_query.reshape(-1), grad_w_key.reshape(-1), grad_w...  27.3 us
    slice x4, local copies, waits for them, and re-layouts, split_flattened(): pieces.append(flattened[offset:offset + width].reshape(shape))  24.7 us
    unnamed x105, local copies, waits for them, and re-layouts  18.5 us
    gather x3, local copies, waits for them, and re-layouts, collect(): tiles = tiles[(jnp.arange(size) - shift) % size]  16.7 us
    ppermute x8, waiting for transfers between devices, collect(): lower.append(lax.ppermute(lower[-1] if lower else x, axis, pairs))  14.6 us
  transfers between devices with their start and end apart: 20, of which 9 were waited for; matrix products, arithmetic and copies ran while one was open for 15% of the time, Pallas kernels for 0%

profile of v1, /device:TPU:0, one launch (start us, length us, event | category | flops | bytes accessed | tf_op | source)
XLA Modules:
  0.0 675.2 jit_solution(13604373827844746288)
XLA Ops:
  8.9 5.0 collective-permute-start.8
  21.6 4.4 collective-permute-start.9
  26.8 2.0 stack.58
  30.0 4.7 collective-permute-done.1
  34.7 2.0 stack.57
  38.7 4.5 collective-permute-start.10
  43.2 75.8 %all-reduce.9.cloned.1.call-done = bf16[885888]{0:T(1024)(128)(2,1)} async-done(((bf16[885888]{0:T(1024)(128)(2,1)}), bf16[885888]{0:T(1024)(128)(2,1)}) %all-reduce.9.cloned.1.call-update) | async-done | bytes 1771792
  128.5 4.5 collective-permute-start.11
  133.0 3.3 collective-permute-done.3
  137.9 4.6 collective-permute-start.12
  142.5 3.3 collective-permute-done.4
  147.2 4.8 collective-permute-start.13
  152.0 3.3 collective-permute-done.5
  155.2 6.3 all_gather.16
  162.2 5.4 all_gather.17
  167.6 5.8 conditional.2
  171.2 2.2 fusion.3
  178.7 2.0 stack.62
  180.7 2.0 stack.55
  184.9 2.0 stack.64
  187.0 2.1 stack.53
  189.1 2.0 stack.65
  195.3 30.0 %stack.67 = bf16[16,165888]{1,0:T(8,128)(2,1)} concatenate(bf16[1,165888]{1,0:T(2,128)(2,1)} %stack.51, bf16[1,165888]{1,0:T(2,128)(2,1)} %stack.52, bf16[1,165888]{1,0:T(2,128)(2,1)} %stack.53, bf16[1,165888]{1,0:T(2,128)(2,1)} %stack.54, bf16[1,165888]{1,0:T(2,128)(2,1)} %stack.55, bf16[1,165888]{1,0:T(2,128)(2,1)} %stack.56, bf16[1,165888]{1,0:T(2,128)(2,1)} %stack.57, ...), dimensions={0} | concatenate | bytes 10616832 | tf_op jit(solution)/shard_map/stack | solution.py:39
  225.3 4.4 fusion.111
  229.8 8.2 %gather_fusion = bf16[16,82944]{1,0:T(8,128)(2,1)} fusion(bf16[16,82944]{1,0:T(8,128)(2,1)} %get-tuple-element.192, s32[1024]{0:T(1024)} %pad_clamp_fusion), kind=kCustom, calls=%fused_computation | custom fusion | bytes 5308480 | tf_op jit(solution)/shard_map/gather | solution.py:41
  238.0 3.5 constant_dynamic-update-slice_fusion.1
  241.5 4.0 gather_fusion.1
  245.5 3.4 constant_dynamic-update-slice_fusion
  248.9 10.2 %slice.103 = bf16[4608,576]{1,0:T(8,128)(2,1)} reshape(bf16[16,165888]{1,0:T(8,128)(2,1)} %constant_dynamic-update-slice_fusion) | data formatting | bytes 10616832 | tf_op jit(solution)/shard_map/slice | solution.py:52
  259.2 11.3 %slice.100 = bf16[1728,1536]{1,0:T(8,128)(2,1)} reshape(bf16[16,165888]{1,0:T(8,128)(2,1)} %constant_dynamic-update-slice_fusion) | data formatting | bytes 10616832 | tf_op jit(solution)/shard_map/slice | solution.py:52
  270.5 2.4 fusion.43
  272.9 2.4 fusion.37
  275.3 2.4 multiply_convert_fusion.1
  282.7 27.5 %conditional.3 = (f32[256,9,64]{0,2,1:T(8,128)}, f32[512,3,64]{0,2,1:T(8,128)}, f32[512,3,64]{0,2,1:T(8,128)}) conditional(s32[]{:T(128)} %convert_element_type.112, () %tuple.30, (bf16[256,9,64]{0,2,1:T(8,128)(2,1)}, bf16[512,3,64]{0,2,1:T(8,128)(2,1)}, bf16[512,3,64]{0,2,1:T(8,128)(2,1)}, bf16[256,576]{0,1:T(8,128)(2,1)S(1)}, ...), branch_computations={%region_7.8_spmd, %region_8.11_spmd} | conditional | flops 254999808 | bytes 9661705 | solution.py:288
  282.7 27.3 %while.13 = (s32[]{:T(128)}, f32[3,256,3,64]{1,3,2,0:T(8,128)}, f32[3,512,64]{1,2,0:T(8,128)}, f32[3,512,64]{1,2,0:T(8,128)}, bf16[3,512,64]{1,2,0:T(8,128)(2,1)...) while((s32[]{:T(128)}, f32[3,256,3,64]{1,3,2,0:T(8,128)}, ...), condition=%wide.region_10.10_spmd, body=%wide.region_9.9_spmd.sunk | while | flops 254999808 | bytes 9661577 | solution.py:169
  311.6 2.7 fusion.83
  319.3 5.3 reshape.331
  324.7 2.4 fusion.117
  327.1 4.7 reshape.330
  331.7 2.4 fusion.116
  334.1 4.5 reshape.329
  338.8 11.2 %pad_maximum_fusion = f32[2654208]{0:T(1024)} fusion(f32[884736]{0:T(1024)} %reshape.331, f32[884736]{0:T(1024)} %reshape.330, f32[884736]{0:T(1024)} %reshape.329), kind=kLoop, calls=%fused_computation.52 | loop fusion | flops 5308416 | bytes 21233664 | tf_op jit(solution)/shard_map/concatenate | solution.py:274
  358.9 27.3 %concatenate.37 = f32[885888]{0:T(1024)} concatenate(f32[331776]{0:T(1024)S(1)} %copy-done.10, f32[110592]{0:T(1024)S(1)} %copy-done.23, f32[110592]{0:T(1024)} %reshape.327, f32[331776]{0:T(1024)} %reshape.328, f32[576]{0:T(1024)S(1)} %get-tuple-element.157, f32[576]{0:T(1024)S(1)} %copy-done.45), dimensions={0} | concatenate | bytes 7087104 | tf_op jit(solution)/shard_map/concatenate | solution.py:338
  388.1 3.1 fusion.58
  392.2 245.2 %all-reduce.13.cloned.1.call-done = (f32[885888]{0:T(1024)}, f32[2654208]{0:T(1024)}) async-done(((f32[885888]{0:T(1024)}, f32[2654208]{0:T(1024)}), (f32[885888]{0:T(1024)}, f32[2654208]{0:T(1024)})) %all-reduce.13.cloned.1.call-update) | async-done | bytes 14160400
  640.6 12.9 %all_gather.19 = f32[165888]{0:T(1024)S(1)} all-gather(f32[82944]{0:T(1024)S(1)} %dynamic-slice.3), channel_id=1, replica_groups=mesh['shard'=16,'ctx'=2] {'ctx'}, dimensions={0}, use_global_device_ids=true | all-gather | bytes 995328 | tf_op jit(solution)/shard_map/all_gather | solution.py:355
  653.6 2.9 multiply_subtract_fusion
  656.4 7.6 %all-reduce.11.cloned.1.call-done = f32[55368]{0:T(1024)} async-done(((f32[55368]{0:T(1024)}), f32[55368]{0:T(1024)}) %all-reduce.11.cloned.1.call-update) | async-done | bytes 221488
  (245 shorter events, 97.3 us)
Async XLA Ops:
  7.2 111.7 %all-reduce.9.cloned.1.call-start = ((), (), s32[]{:S(2)}) async-start(), calls=%async_computation.4 | async-start | bytes 3547136
  8.3 13.2 %collective-permute-start = (bf16[165888]{0:T(1024)(128)(2,1)S(1)}, bf16[165888]{0:T(1024)(128)(2,1)}, u32[]{:S(2)}, u32[]{:S(2)}) collective-permute-start(bf16[165888]{0:T(1024)(128)(2,1)S(1)} %convert_element_type.123), channel_id=1, source_target_pairs={{0,2},{2,4},{4,6},{6,8},{8,10},{10,12},{12,14},{14,16},{16,18},{18... | collective-permute-start | bytes 995336 | tf_op jit(solution)/shard_map/ppermute | solution.py:36
  8.9 12.7 %collective-permute-start.8 = (bf16[165888]{0:T(1024)(128)(2,1)S(1)}, bf16[165888]{0:T(1024)(128)(2,1)S(1)}, u32[]{:S(2)}, u32[]{:S(2)}) collective-permute-start(bf16[165888]{0:T(1024)(128)(2,1)S(1)} %convert_element_type.123), channel_id=1, source_target_pairs={{2,0},{4,2},{6,4},{8,6},{10,8},{12,10},{14,12},{16,14},{18,16},{20... | collective-permute-start | bytes 995336 | tf_op jit(solution)/shard_map/ppermute | solution.py:38
  13.9 7.5 %copy-start = (bf16[256,576]{0,1:T(8,128)(2,1)S(1)}, bf16[256,576]{0,1:T(8,128)(2,1)}, u32[]{:S(2)}) copy-start(bf16[256,576]{0,1:T(8,128)(2,1)} %param.15) | copy-start | bytes 884740
  19.4 330.6 %reduce-scatter.3.cloned.1.call-start = ((), (), s32[]{:S(2)}) async-start(), calls=%async_computation.2 | async-start | bytes 589824 | tf_op jit(solution)/shard_map/reduce_scatter | solution.py:300
  20.7 125.1 %copy-start.24 = (f32[256,64]{0,1:T(8,128)}, f32[256,64]{0,1:T(8,128)S(1)}, u32[]{:S(2)}) copy-start(f32[256,64]{0,1:T(8,128)S(1)} %get-tuple-element.210) | copy-start | bytes 196612
  20.7 289.5 %copy-start.27 = (f32[256,64]{0,1:T(8,128)}, f32[256,64]{0,1:T(8,128)S(1)}, u32[]{:S(2)}) copy-start(f32[256,64]{0,1:T(8,128)S(1)} %get-tuple-element.211) | copy-start | bytes 196612
  21.5 13.2 %collective-permute-start.1 = (bf16[165888]{0:T(1024)(128)(2,1)}, bf16[165888]{0:T(1024)(128)(2,1)}, u32[]{:S(2)}, u32[]{:S(2)}) collective-permute-start(bf16[165888]{0:T(1024)(128)(2,1)} %collective-permute-done), channel_id=1, source_target_pairs={{0,2},{2,4},{4,6},{6,8},{8,10},{10,12},{12,14},{14,16},{16,18},{18... | collective-permute-start | bytes 995336 | tf_op jit(solution)/shard_map/ppermute | solution.py:36
  21.6 15.1 %collective-permute-start.9 = (bf16[165888]{0:T(1024)(128)(2,1)S(1)}, bf16[165888]{0:T(1024)(128)(2,1)}, u32[]{:S(2)}, u32[]{:S(2)}) collective-permute-start(bf16[165888]{0:T(1024)(128)(2,1)S(1)} %collective-permute-done.8), channel_id=1, source_target_pairs={{2,0},{4,2},{6,4},{8,6},{10,8},{12,10},{14,12},{16,14},{18,16},{20... | collective-permute-start | bytes 995336 | tf_op jit(solution)/shard_map/ppermute | solution.py:38
  34.7 91.8 %collective-permute-start.2 = (bf16[165888]{0:T(1024)(128)(2,1)}, bf16[165888]{0:T(1024)(128)(2,1)}, u32[]{:S(2)}, u32[]{:S(2)}) collective-permute-start(bf16[165888]{0:T(1024)(128)(2,1)} %collective-permute-done.1), channel_id=1, source_target_pairs={{0,2},{2,4},{4,6},{6,8},{8,10},{10,12},{12,14},{14,16},{16,18},{18... | collective-permute-start | bytes 995336 | tf_op jit(solution)/shard_map/ppermute | solution.py:36
  38.7 89.8 %collective-permute-start.10 = (bf16[165888]{0:T(1024)(128)(2,1)}, bf16[165888]{0:T(1024)(128)(2,1)}, u32[]{:S(2)}, u32[]{:S(2)}) collective-permute-start(bf16[165888]{0:T(1024)(128)(2,1)} %collective-permute-done.9), channel_id=1, source_target_pairs={{2,0},{4,2},{6,4},{8,6},{10,8},{12,10},{14,12},{16,14},{18,16},{20... | collective-permute-start | bytes 995336 | tf_op jit(solution)/shard_map/ppermute | solution.py:38
  126.5 9.7 %collective-permute-start.3 = (bf16[165888]{0:T(1024)(128)(2,1)}, bf16[165888]{0:T(1024)(128)(2,1)}, u32[]{:S(2)}, u32[]{:S(2)}) collective-permute-start(bf16[165888]{0:T(1024)(128)(2,1)} %collective-permute-done.2), channel_id=1, source_target_pairs={{0,2},{2,4},{4,6},{6,8},{8,10},{10,12},{12,14},{14,16},{16,18},{18... | collective-permute-start | bytes 995336 | tf_op jit(solution)/shard_map/ppermute | solution.py:36
  127.6 18.2 %copy-start.7 = (bf16[576,576]{1,0:T(8,128)(2,1)}, bf16[576,576]{1,0:T(8,128)(2,1)S(1)}, u32[]{:S(2)}) copy-start(bf16[576,576]{1,0:T(8,128)(2,1)S(1)} %reshape.314) | copy-start | bytes 1990660
  128.5 9.4 %collective-permute-start.11 = (bf16[165888]{0:T(1024)(128)(2,1)}, bf16[165888]{0:T(1024)(128)(2,1)S(1)}, u32[]{:S(2)}, u32[]{:S(2)}) collective-permute-start(bf16[165888]{0:T(1024)(128)(2,1)} %collective-permute-done.10), channel_id=1, source_target_pairs={{2,0},{4,2},{6,4},{8,6},{10,8},{12,10},{14,12},{16,14},{18,16},{20... | collective-permute-start | bytes 995336 | tf_op jit(solution)/shard_map/ppermute | solution.py:38
  136.2 9.6 %collective-permute-start.4 = (bf16[165888]{0:T(1024)(128)(2,1)}, bf16[165888]{0:T(1024)(128)(2,1)S(1)}, u32[]{:S(2)}, u32[]{:S(2)}) collective-permute-start(bf16[165888]{0:T(1024)(128)(2,1)} %collective-permute-done.3), channel_id=1, source_target_pairs={{0,2},{2,4},{4,6},{6,8},{8,10},{10,12},{12,14},{14,16},{16,18},{18... | collective-permute-start | bytes 995336 | tf_op jit(solution)/shard_map/ppermute | solution.py:36
  136.3 31.3 %copy-start.29 = (pred[256,512]{0,1:T(8,128)(4,1)S(1)}, pred[256,512]{0,1:T(8,128)(4,1)}, u32[]{:S(2)}) copy-start(pred[256,512]{0,1:T(8,128)(4,1)} %fusion.78) | copy-start | bytes 393220
  137.9 23.7 %copy-start.39 = (bf16[165888]{0:T(1024)(128)(2,1)}, bf16[165888]{0:T(1024)(128)(2,1)S(1)}, u32[]{:S(2)}) copy-start(bf16[165888]{0:T(1024)(128)(2,1)S(1)} %collective-permute-done.11) | copy-start | bytes 995332
  137.9 9.2 %collective-permute-start.12 = (bf16[165888]{0:T(1024)(128)(2,1)S(1)}, bf16[165888]{0:T(1024)(128)(2,1)}, u32[]{:S(2)}, u32[]{:S(2)}) collective-permute-start(bf16[165888]{0:T(1024)(128)(2,1)S(1)} %collective-permute-done.11), channel_id=1, source_target_pairs={{2,0},{4,2},{6,4},{8,6},{10,8},{12,10},{14,12},{16,14},{18,16},{20... | collective-permute-start | bytes 995336 | tf_op jit(solution)/shard_map/ppermute | solution.py:38
  145.8 15.8 %copy-start.41 = (bf16[165888]{0:T(1024)(128)(2,1)}, bf16[165888]{0:T(1024)(128)(2,1)S(1)}, u32[]{:S(2)}) copy-start(bf16[165888]{0:T(1024)(128)(2,1)S(1)} %collective-permute-done.4) | copy-start | bytes 995332
  145.8 9.4 %collective-permute-start.5 = (bf16[165888]{0:T(1024)(128)(2,1)S(1)}, bf16[165888]{0:T(1024)(128)(2,1)}, u32[]{:S(2)}, u32[]{:S(2)}) collective-permute-start(bf16[165888]{0:T(1024)(128)(2,1)S(1)} %collective-permute-done.4), channel_id=1, source_target_pairs={{0,2},{2,4},{4,6},{6,8},{8,10},{10,12},{12,14},{14,16},{16,18},{18... | collective-permute-start | bytes 995336 | tf_op jit(solution)/shard_map/ppermute | solution.py:36
  147.2 26.7 %collective-permute-start.13 = (bf16[165888]{0:T(1024)(128)(2,1)}, bf16[165888]{0:T(1024)(128)(2,1)}, u32[]{:S(2)}, u32[]{:S(2)}) collective-permute-start(bf16[165888]{0:T(1024)(128)(2,1)} %collective-permute-done.12), channel_id=1, source_target_pairs={{2,0},{4,2},{6,4},{8,6},{10,8},{12,10},{14,12},{16,14},{18,16},{20... | collective-permute-start | bytes 995336 | tf_op jit(solution)/shard_map/ppermute | solution.py:38
  155.2 20.2 %collective-permute-start.6 = (bf16[165888]{0:T(1024)(128)(2,1)}, bf16[165888]{0:T(1024)(128)(2,1)}, u32[]{:S(2)}, u32[]{:S(2)}) collective-permute-start(bf16[165888]{0:T(1024)(128)(2,1)} %collective-permute-done.5), channel_id=1, source_target_pairs={{0,2},{2,4},{4,6},{6,8},{8,10},{10,12},{12,14},{14,16},{16,18},{18... | collective-permute-start | bytes 995336 | tf_op jit(solution)/shard_map/ppermute | solution.py:36
  162.2 11.2 %copy-start.5 = (bf16[576,576]{1,0:T(8,128)(2,1)}, bf16[576,576]{1,0:T(8,128)(2,1)S(1)}, u32[]{:S(2)}) copy-start(bf16[576,576]{1,0:T(8,128)(2,1)S(1)} %reshape.320) | copy-start | bytes 1990660
  173.4 9.4 %copy-start.40 = (bf16[165888]{0:T(1024)(128)(2,1)S(1)}, bf16[165888]{0:T(1024)(128)(2,1)}, u32[]{:S(2)}) copy-start(bf16[165888]{0:T(1024)(128)(2,1)} %copy-done.39) | copy-start | bytes 995332
  173.8 11.1 %copy-start.11 = (f32[256,576]{0,1:T(8,128)}, f32[256,576]{0,1:T(8,128)S(1)}, u32[]{:S(2)}) copy-start(f32[256,576]{0,1:T(8,128)S(1)} %get-tuple-element.213) | copy-start | bytes 1769476
  173.8 10.0 %copy-start.42 = (bf16[165888]{0:T(1024)(128)(2,1)S(1)}, bf16[165888]{0:T(1024)(128)(2,1)}, u32[]{:S(2)}) copy-start(bf16[165888]{0:T(1024)(128)(2,1)} %copy-done.41) | copy-start | bytes 995332
  173.9 19.2 %collective-permute-start.14 = (bf16[165888]{0:T(1024)(128)(2,1)}, bf16[165888]{0:T(1024)(128)(2,1)S(1)}, u32[]{:S(2)}, u32[]{:S(2)}) collective-permute-start(bf16[165888]{0:T(1024)(128)(2,1)} %collective-permute-done.13), channel_id=1, source_target_pairs={{2,0},{4,2},{6,4},{8,6},{10,8},{12,10},{14,12},{16,14},{18,16},{20... | collective-permute-start | bytes 995336 | tf_op jit(solution)/shard_map/ppermute | solution.py:38
  175.4 18.8 %collective-permute-start.7 = (bf16[165888]{0:T(1024)(128)(2,1)}, bf16[165888]{0:T(1024)(128)(2,1)S(1)}, u32[]{:S(2)}, u32[]{:S(2)}) collective-permute-start(bf16[165888]{0:T(1024)(128)(2,1)} %collective-permute-done.6), channel_id=1, source_target_pairs={{0,2},{2,4},{4,6},{6,8},{8,10},{10,12},{12,14},{14,16},{16,18},{18... | collective-permute-start | bytes 995336 | tf_op jit(solution)/shard_map/ppermute | solution.py:36
  187.0 8.3 %copy-start.16 = (bf16[1,165888]{1,0:T(2,128)(2,1)S(1)}, bf16[1,165888]{1,0:T(2,128)(2,1)}, u32[]{:S(2)}) copy-start(bf16[1,165888]{1,0:T(2,128)(2,1)} %stack.58) | copy-start | bytes 995332
  187.0 8.3 %copy-start.17 = (bf16[1,165888]{1,0:T(2,128)(2,1)S(1)}, bf16[1,165888]{1,0:T(2,128)(2,1)}, u32[]{:S(2)}) copy-start(bf16[1,165888]{1,0:T(2,128)(2,1)} %stack.60) | copy-start | bytes 995332
  259.1 11.3 %copy-start.14 = (bf16[256,576]{0,1:T(8,128)(2,1)S(1)}, bf16[256,576]{0,1:T(8,128)(2,1)}, u32[]{:S(2)}) copy-start(bf16[256,576]{0,1:T(8,128)(2,1)} %multiply_convert_fusion.3) | copy-start | bytes 884740
  259.2 13.7 %copy-start.19 = (bf16[256,576]{0,1:T(8,128)(2,1)S(1)}, bf16[256,576]{0,1:T(8,128)(2,1)}, u32[]{:S(2)}) copy-start(bf16[256,576]{0,1:T(8,128)(2,1)} %param.16) | copy-start | bytes 884740
  270.5 4.8 copy-start.1
  310.2 44.7 %reduce-scatter.5.cloned.1.call-start = ((), (), s32[]{:S(2)}) async-start(), calls=%async_computation.3 | async-start | bytes 589824 | tf_op jit(solution)/shard_map/reduce_scatter | solution.py:306
  319.3 5.4 copy-start.15
  319.3 5.4 copy-start.36
  327.1 4.7 copy-start.34
  338.7 11.3 %copy-start.28 = (f32[256,64]{0,1:T(8,128)S(1)}, f32[256,64]{0,1:T(8,128)}, u32[]{:S(2)}) copy-start(f32[256,64]{0,1:T(8,128)} %copy-done.27) | copy-start | bytes 196612
  338.7 12.4 %copy-start.26 = (f32[256,64]{0,1:T(8,128)S(1)}, f32[256,64]{0,1:T(8,128)}, u32[]{:S(2)}) copy-start(f32[256,64]{0,1:T(8,128)} %copy-done.24) | copy-start | bytes 196612
  338.7 298.7 %all-reduce.13.cloned.1.call-start = ((), (), s32[]{:S(2)}) async-start(), calls=%async_computation.6 | async-start | bytes 28327936
  353.7 5.2 copy-start.10
  353.7 5.2 copy-start.45
  386.3 5.0 copy-start.3
  386.3 277.8 %all-reduce.11.cloned.1.call-start = ((), (), s32[]{:S(2)}) async-start(), calls=%async_computation.5 | async-start | bytes 450560
  391.3 262.3 %copy-start.18 = (f32[165888]{0:T(1024)S(1)}, f32[165888]{0:T(1024)}, u32[]{:S(2)}) copy-start(f32[165888]{0:T(1024)} %param.21) | copy-start | bytes 1990660
  640.6 23.4 %copy-start.31 = (f32[55368]{0:T(1024)S(1)}, f32[55368]{0:T(1024)}, u32[]{:S(2)}) copy-start(f32[55368]{0:T(1024)} %param.18) | copy-start | bytes 664420
  640.6 23.4 %copy-start.43 = (f32[55368]{0:T(1024)S(1)}, f32[55368]{0:T(1024)}, u32[]{:S(2)}) copy-start(f32[55368]{0:T(1024)} %param.19) | copy-start | bytes 664420
  640.6 23.4 %copy-start.44 = (f32[55368]{0:T(1024)S(1)}, f32[55368]{0:T(1024)}, u32[]{:S(2)}) copy-start(f32[55368]{0:T(1024)} %param.20) | copy-start | bytes 664420
  (19 other events, 41.7 us)
Sparse Core Ops, SparseCore 0:
  19.5 99.3 all-reduce.8
  310.3 14.2 reduce-scatter.2
  338.8 14.3 reduce-scatter.4
  386.4 250.9 all-reduce.12
  640.1 23.8 all-reduce.10
